TPU v7x, 32 devices: a whole 2x2x4 slice. The times are simulated.
32 devices in a mesh: row: 4 (over y, core), col: 8 (over z, x).
Axes of the slice: x: 2, y: 2, z: 4, core: 2. Of those that a mesh axis runs over, the one named last changes fastest.
Arguments:
- ancestor_inverse: float32 [12288, 12288], P('row', 'col')
- factor: bfloat16 [3, 12288, 512], P(None, ('row', 'col')), may hold values from -0.5 to 0.5
- coupling: float32 [3, 512, 512], replicated, may hold values from -0.25 to 0.25
- diagonal_inverse: float32 [3, 512, 512], replicated, may hold values from -6 to 6
- ancestors: int32 [3, 24], replicated, may hold values from -1 to 23, as said below
Outputs:
- block_columns: float32 [3, 12288, 512], P(None, ('row', 'col'))
- block_rows: float32 [3, 12288, 512], P(None, ('col', 'row'))
- node_blocks: float32 [3, 3, 512, 512], replicated
Inputs may be any that keep to these rules, and one draw needn't show every extreme that they name: `ancestors`: row k lists the ancestor block rows of supernode k, blocks of 512 rows: distinct indices in increasing order, then -1 in the slots left. Every block is listed by some supernode.
All inputs are finite; a program needn't handle non-finite values.
Results may differ from a plain program's by a relative error of at most 0.0003.
Values may be sent and summed in bfloat16 or wider, within the bound.
No kernel may reach another device: no remote copies, remote signals or barrier semaphores. Data moves between devices by JAX's collectives and lax.ppermute only.
A program may use at most 128 MiB of HBM per device.

v0:
```python
import jax
import jax.numpy as jnp
from jax import lax
from jax.sharding import PartitionSpec as P

highest = lax.Precision.HIGHEST


def broadcast(value, axis, source):
    kept = jnp.where(lax.axis_index(axis) == source, value, 0).astype(value.dtype)
    return lax.psum(kept, axis)


def matmul(left, right):
    return jnp.dot(left, right, precision=highest)


def left_dot(left, right):
    return lax.dot_general(left, right, (((0,), (0,)), ((), ())), precision=highest)


def pair_index(later, earlier):
    return later * (later - 1) // 2 + earlier


def local(ancestor_inverse, factor, coupling, diagonal_inverse, ancestors):
    col_count = lax.axis_size("col")
    row_index = lax.axis_index("row")
    col_index = lax.axis_index("col")
    nodes_total, piece_rows, sn_width = factor.shape
    rows_here, cols_here = ancestor_inverse.shape
    group_ratio = rows_here // cols_here
    first_row = (row_index * col_count + col_index) * piece_rows
    block_of_row = (first_row + jnp.arange(piece_rows, dtype=jnp.int32)) // sn_width
    source_row = col_index // group_ratio
    block_start = col_index % group_ratio * cols_here
    row_layout = []
    col_layout = []
    solved = {}
    for current in range(nodes_total):
        listed = jnp.any(ancestors[current][:, None] == block_of_row[None, :], axis=0)
        lower_part = jnp.where(listed[:, None], factor[current], jnp.zeros_like(factor[current]))
        lower_rows = lax.all_gather(lower_part, "col", axis=0, tiled=True)
        own_block = lax.dynamic_slice_in_dim(lower_rows, block_start, cols_here, 0)
        lower_cols = broadcast(own_block, "row", source_row).astype(jnp.float32)
        lower_here = lower_part.astype(jnp.float32)
        product_sum = lax.psum_scatter(
            matmul(ancestor_inverse, lower_cols), "col", scatter_dimension=0, tiled=True
        )
        for earlier in range(current):
            product_sum = product_sum + matmul(
                row_layout[earlier], coupling[pair_index(current, earlier)]
            )
        column = -product_sum
        stacked = jnp.concatenate(row_layout + [column], axis=1)
        summed = lax.psum(left_dot(lower_here, stacked), ("row", "col"))
        crosses = [
            summed[:, earlier * sn_width : (earlier + 1) * sn_width] for earlier in range(current)
        ]
        self_term = summed[:, current * sn_width : (current + 1) * sn_width]
        for earlier in range(current):
            block_value = -crosses[earlier].T
            for inner in range(current):
                block_value = block_value - matmul(
                    solved[earlier, inner], coupling[pair_index(current, inner)]
                )
            solved[earlier, current] = block_value
            solved[current, earlier] = block_value.T
        diag_value = diagonal_inverse[current] - self_term
        for earlier in range(current):
            diag_value = diag_value - left_dot(
                coupling[pair_index(current, earlier)], solved[earlier, current]
            )
        solved[current, current] = diag_value
        rows_float = lower_rows.astype(jnp.float32)
        mirror = lax.psum_scatter(
            left_dot(ancestor_inverse, rows_float), "row", scatter_dimension=0, tiled=True
        )
        for earlier in range(current):
            mirror = mirror + matmul(col_layout[earlier], coupling[pair_index(current, earlier)])
        col_layout.append(-mirror)
        row_layout.append(column)
    finished = jnp.stack(row_layout)
    mirrored_all = jnp.stack(col_layout)
    node_blocks = jnp.stack(
        [
            jnp.stack([solved[first_node, second_node] for second_node in range(nodes_total)])
            for first_node in range(nodes_total)
        ]
    )
    return (finished, mirrored_all, node_blocks)


def solution(mesh):
    placed = (P("row", "col"), P(None, ("row", "col"), None), P(), P(), P())
    return jax.shard_map(
        local,
        mesh=mesh,
        in_specs=placed,
        out_specs=(P(None, ("row", "col"), None), P(None, ("col", "row"), None), P()),
        check_vma=False,
    )
```

profile of v0, /device:TPU:0, one launch (start us, length us, event | category | flops | bytes accessed | tf_op | source)
XLA Modules:
  0.0 1007.5 jit_solution(5974017174490358877)
XLA Ops:
  8.1 2.5 bitcast_select_fusion.1
  12.2 61.3 %all-gather.8.cloned.1.call-done = bf16[3072,512]{1,0:T(8,128)(2,1)} async-done(((bf16[384,512]{1,0:T(8,128)(2,1)}), bf16[3072,512]{1,0:T(8,128)(2,1)}) %all-gather.8.cloned.1.call-update) | async-done | bytes 3145744 | tf_op jit(solution)/shard_map/all_gather | solution.py:43
  73.6 2.8 dynamic-slice_select_fusion
  76.4 58.1 %all-gather.4.cloned.1.call-done = bf16[3072,512]{1,0:T(8,128)(2,1)} async-done(((bf16[384,512]{1,0:T(8,128)(2,1)}), bf16[3072,512]{1,0:T(8,128)(2,1)}) %all-gather.4.cloned.1.call-update) | async-done | bytes 3145744 | tf_op jit(solution)/shard_map/all_gather | solution.py:43
  134.5 2.8 dynamic-slice_select_fusion.2
  137.3 58.1 %all-gather.6.cloned.1.call-done = bf16[3072,512]{1,0:T(8,128)(2,1)} async-done(((bf16[384,512]{1,0:T(8,128)(2,1)}), bf16[3072,512]{1,0:T(8,128)(2,1)}) %all-gather.6.cloned.1.call-update) | async-done | bytes 3145744 | tf_op jit(solution)/shard_map/all_gather | solution.py:43
  195.4 2.8 dynamic-slice_select_fusion.1
  198.3 92.8 %all-reduce.7.cloned.1.call-done = (bf16[1536,512]{1,0:T(8,128)(2,1)}, bf16[1536,512]{1,0:T(8,128)(2,1)}, bf16[1536,512]{1,0:T(8,128)(2,1)}) async-done(((bf16[1536,512]{1,0:T(8,128)(2,1)}, bf16[1536,512]{1,0:T(8,128)(2,1)}, bf16[1536,512]{1,0:T(8,128)(2,1)}), (bf16[1536,512]{1,0:T(8,128)(2,1)}, bf16[1536,512]{1,0:T(8,128)(2,1)}, bf16[1536,512]{1,0:T(8,128)(2,1)})) %all-reduce.7.cloned.1.call-update) | async-done | bytes 4718608 | tf_op jit(solution)/shard_map/psum | solution.py:11
  291.1 22.4 %convolution_bitcast_fusion.2 = f32[3072,512]{0,1:T(8,128)} fusion(bf16[1536,512]{1,0:T(8,128)(2,1)} %get-tuple-element.16, f32[3072,1536]{1,0:T(8,128)} %param.5), kind=kOutput, calls=%fused_computation.3 | convolution fusion | flops 28991029248 | bytes 26738688 | tf_op jit(solution)/shard_map/dot_general | solution.py:15
  314.9 21.8 %convolution_bitcast_fusion.1 = f32[3072,512]{0,1:T(8,128)} fusion(bf16[1536,512]{1,0:T(8,128)(2,1)S(1)} %copy-done.30, f32[3072,1536]{1,0:T(8,128)} %param.5), kind=kOutput, calls=%fused_computation.2 | convolution fusion | flops 28991029248 | bytes 26738688 | tf_op jit(solution)/shard_map/dot_general | solution.py:15
  338.1 21.8 %convolution_bitcast_fusion = f32[3072,512]{0,1:T(8,128)} fusion(bf16[1536,512]{1,0:T(8,128)(2,1)S(1)} %copy-done.29, f32[3072,1536]{1,0:T(8,128)} %param.5), kind=kOutput, calls=%fused_computation.1 | convolution fusion | flops 28991029248 | bytes 26738688 | tf_op jit(solution)/shard_map/dot_general | solution.py:15
  361.8 19.7 %convolution_bitcast_fusion.3 = f32[1536,512]{0,1:T(8,128)} fusion(bf16[3072,512]{1,0:T(8,128)(2,1)S(1)} %copy-done.28, f32[3072,1536]{1,0:T(8,128)} %param.5), kind=kOutput, calls=%fused_computation.4 | convolution fusion | flops 28991029248 | bytes 25165824 | tf_op jit(solution)/shard_map/dot_general | solution.py:19
  383.5 19.9 %convolution_bitcast_fusion.5 = f32[1536,512]{0,1:T(8,128)} fusion(bf16[3072,512]{1,0:T(8,128)(2,1)S(1)} %copy-done.27, f32[3072,1536]{1,0:T(8,128)} %param.5), kind=kOutput, calls=%fused_computation.6 | convolution fusion | flops 28991029248 | bytes 25165824 | tf_op jit(solution)/shard_map/dot_general | solution.py:19
  405.3 19.7 %convolution_bitcast_fusion.4 = f32[1536,512]{0,1:T(8,128)} fusion(bf16[3072,512]{1,0:T(8,128)(2,1)S(1)} %copy-done.26, f32[3072,1536]{1,0:T(8,128)} %param.5), kind=kOutput, calls=%fused_computation.5 | convolution fusion | flops 28991029248 | bytes 25165824 | tf_op jit(solution)/shard_map/dot_general | solution.py:19
  425.3 6.5 reduce-scatter.7.cloned.1.call-done
  431.8 2.4 fusion.73
  434.2 3.3 fusion.64
  437.5 115.1 %reduce-scatter.9.cloned.1.call-done = f32[384,512]{0,1:T(8,128)} async-done(((f32[3072,512]{0,1:T(8,128)}), f32[384,512]{0,1:T(8,128)}) %reduce-scatter.9.cloned.1.call-update) | async-done | bytes 786448 | tf_op jit(solution)/shard_map/reduce_scatter | solution.py:47
  552.6 3.4 fusion.14
  556.9 3.1 fusion.6
  560.0 114.0 %reduce-scatter.11.cloned.1.call-done = f32[384,512]{0,1:T(8,128)} async-done(((f32[3072,512]{0,1:T(8,128)}), f32[384,512]{0,1:T(8,128)}) %reduce-scatter.11.cloned.1.call-update) | async-done | bytes 786448 | tf_op jit(solution)/shard_map/reduce_scatter | solution.py:47
  674.0 3.3 convolution_add_fusion.4
  680.2 4.5 fusion
  684.7 2.3 slice.74
  687.0 2.9 copy.65
  690.0 23.6 %reduce-scatter.17.cloned.1.call-done = f32[384,512]{0,1:T(8,128)} async-done(((f32[1536,512]{0,1:T(8,128)}), f32[384,512]{0,1:T(8,128)}) %reduce-scatter.17.cloned.1.call-update) | async-done | bytes 786448 | tf_op jit(solution)/shard_map/reduce_scatter | solution.py:76
  713.6 40.3 %reduce-scatter.13.cloned.1.call-done = f32[384,512]{0,1:T(8,128)} async-done(((f32[1536,512]{0,1:T(8,128)}), f32[384,512]{0,1:T(8,128)}) %reduce-scatter.13.cloned.1.call-update) | async-done | bytes 786448 | tf_op jit(solution)/shard_map/reduce_scatter | solution.py:76
  753.9 4.1 convolution_add_fusion.1
  758.0 36.0 %reduce-scatter.15.cloned.1.call-done = f32[384,512]{0,1:T(8,128)} async-done(((f32[1536,512]{0,1:T(8,128)}), f32[384,512]{0,1:T(8,128)}) %reduce-scatter.15.cloned.1.call-update) | async-done | bytes 786448 | tf_op jit(solution)/shard_map/reduce_scatter | solution.py:76
  794.0 3.4 fusion.16
  800.9 3.0 copy.51
  804.0 3.2 pad_maximum_fusion.1
  807.1 3.2 copy.50
  810.3 146.5 %all-reduce.5.cloned.1.call-done = (f32[512,1536]{1,0:T(8,128)}, f32[512,512]{1,0:T(8,128)}, f32[512,1024]{0,1:T(8,128)}) async-done(((f32[512,1536]{1,0:T(8,128)}, f32[512,512]{1,0:T(8,128)}, f32[512,1024]{0,1:T(8,128)}), (f32[512,1536]{1,0:T(8,128)}, f32[512,512]{1,0:T(8,128)}, f32[512,1024]{0,1:T(8,128)})) %all-reduce.5.cloned.1.call-update) | async-done | bytes 6291472 | tf_op jit(solution)/shard_map/psum | solution.py:56
  956.9 3.6 fusion.34
  960.5 3.2 bitcast_subtract_fusion.7
  963.7 1.9 fusion.32
  967.5 2.0 fusion.13
  970.5 1.9 fusion.25
  972.4 3.3 fusion.12
  975.7 2.3 fusion.20
  978.0 2.3 fusion.70
  980.3 2.5 copy.39
  982.9 5.3 fusion.11
  988.2 2.0 maximum_bitcast_fusion.1
  990.1 2.4 copy.49
  992.6 2.3 maximum_bitcast_fusion.2
  995.6 5.1 pad_maximum_fusion
  (93 shorter events, 22.2 us)
Async XLA Ops:
  7.2 66.4 %all-gather.8.cloned.1.call-start = ((), (), s32[]{:S(2)}) async-start(), calls=%async_computation.10 | async-start | bytes 3538944 | tf_op jit(solution)/shard_map/all_gather | solution.py:43
  10.7 123.8 %all-gather.4.cloned.1.call-start = ((), (), s32[]{:S(2)}) async-start(), calls=%async_computation.6 | async-start | bytes 3538944 | tf_op jit(solution)/shard_map/all_gather | solution.py:43
  11.4 183.9 %all-gather.6.cloned.1.call-start = ((), (), s32[]{:S(2)}) async-start(), calls=%async_computation.8 | async-start | bytes 3538944 | tf_op jit(solution)/shard_map/all_gather | solution.py:43
  12.2 278.9 %all-reduce.7.cloned.1.call-start = ((), (), s32[]{:S(2)}) async-start(), calls=%async_computation.16 | async-start | bytes 9437184 | tf_op jit(solution)/shard_map/psum | solution.py:11
  198.2 233.6 %reduce-scatter.7.cloned.1.call-start = ((), (), s32[]{:S(2)}) async-start(), calls=%async_computation.7 | async-start | bytes 7077888 | tf_op jit(solution)/shard_map/reduce_scatter | solution.py:47
  313.5 1.4 copy-start.30
  313.5 239.1 %reduce-scatter.9.cloned.1.call-start = ((), (), s32[]{:S(2)}) async-start(), calls=%async_computation.9 | async-start | bytes 7077888 | tf_op jit(solution)/shard_map/reduce_scatter | solution.py:47
  336.7 1.4 copy-start.29
  336.7 337.3 %reduce-scatter.11.cloned.1.call-start = ((), (), s32[]{:S(2)}) async-start(), calls=%async_computation.11 | async-start | bytes 7077888 | tf_op jit(solution)/shard_map/reduce_scatter | solution.py:47
  359.9 1.9 copy-start.28
  359.9 353.6 %reduce-scatter.17.cloned.1.call-start = ((), (), s32[]{:S(2)}) async-start(), calls=%async_computation.14 | async-start | bytes 3932160 | tf_op jit(solution)/shard_map/reduce_scatter | solution.py:76
  381.6 2.0 copy-start.27
  381.6 372.2 %reduce-scatter.13.cloned.1.call-start = ((), (), s32[]{:S(2)}) async-start(), calls=%async_computation.12 | async-start | bytes 3932160 | tf_op jit(solution)/shard_map/reduce_scatter | solution.py:76
  403.4 1.9 copy-start.26
  403.5 390.5 %reduce-scatter.15.cloned.1.call-start = ((), (), s32[]{:S(2)}) async-start(), calls=%async_computation.13 | async-start | bytes 3932160 | tf_op jit(solution)/shard_map/reduce_scatter | solution.py:76
  425.0 9.2 copy-start.23
  425.0 127.6 %copy-start = (f32[3,512,512]{2,1,0:T(8,128)S(1)}, f32[3,512,512]{2,1,0:T(8,128)}, u32[]{:S(2)}) copy-start(f32[3,512,512]{2,1,0:T(8,128)} %param.7) | copy-start | bytes 9437188
  425.0 531.9 %all-reduce.5.cloned.1.call-start = ((), (), s32[]{:S(2)}) async-start(), calls=%async_computation.15 | async-start | bytes 12582912 | tf_op jit(solution)/shard_map/psum | solution.py:56
  437.5 119.4 %copy-start.24 = (bf16[384,512]{1,0:T(8,128)(2,1)S(1)}, bf16[384,512]{1,0:T(8,128)(2,1)}, u32[]{:S(2)}) copy-start(bf16[384,512]{1,0:T(8,128)(2,1)} %get-tuple-element.22) | copy-start | bytes 1179652
  552.6 4.3 copy-start.13
  555.9 0.9 copy-start.3
  560.0 120.2 %copy-start.16 = (bf16[384,512]{1,0:T(8,128)(2,1)S(1)}, bf16[384,512]{1,0:T(8,128)(2,1)}, u32[]{:S(2)}) copy-start(bf16[384,512]{1,0:T(8,128)(2,1)} %get-tuple-element.24) | copy-start | bytes 1179652
  674.0 3.4 copy-start.4
  674.0 6.2 copy-start.14
  679.2 0.9 copy-start.12
  794.0 3.4 copy-start.25
  794.0 5.3 copy-start.15
  956.9 3.6 copy-start.10
  956.9 3.6 copy-start.11
  963.7 3.8 copy-start.1
  963.7 3.8 copy-start.17
  963.7 3.8 copy-start.18
  965.6 12.4 %copy-start.5 = (f32[512,512]{0,1:T(8,128)}, f32[512,512]{0,1:T(8,128)S(1)}, u32[]{:S(2)}) copy-start(f32[512,512]{0,1:T(8,128)S(1)} %fusion.32) | copy-start | bytes 3145732
  967.5 4.9 copy-start.7
  969.5 1.0 copy-start.8
  972.4 5.6 copy-start.6
  982.9 5.3 copy-start.9
  982.9 5.3 copy-start.21
  982.9 5.3 copy-start.22
  992.5 2.4 copy-start.2
  992.5 2.5 copy-start.19
  992.5 2.8 copy-start.20
Sparse Core Ops, SparseCore 0:
  10.8 62.7 all-gather.7
  75.7 58.6 all-gather.3
  136.7 58.6 all-gather.5
  198.3 92.7 all-reduce.6
  313.6 118.1 reduce-scatter.6
  435.2 117.2 reduce-scatter.8
  556.7 117.2 reduce-scatter.10
  676.5 36.9 reduce-scatter.16
  716.1 37.7 reduce-scatter.12
  756.2 37.7 reduce-scatter.14
  800.5 156.3 all-reduce.4
where the time goes:
time: 1020 us; the launch traced here: 1010 us
  waiting for transfers between devices  754 us (74%)
  matrix products  177 us (17%)
  other arithmetic  32.6 us (3%)
  local copies, waits for them, and re-layouts  28.1 us (3%)
  between operations  14.5 us (1%)
    reduce_scatter x3, waiting for transfers between devices, local(): lax.psum_scatter(matmul(ancestor_inverse, lower_cols), 'col', scatter_dim...  236 us
    all_gather x3, waiting for transfers between devices, local(): lower_rows = lax.all_gather(lower_part, 'col', axis=0, tiled=True)  177 us
    psum x1, waiting for transfers between devices, local(): summed = lax.psum(left_dot(lower_here, stacked), ('row', 'col'))  147 us
    reduce_scatter x3, waiting for transfers between devices, local(): lax.psum_scatter(left_dot(ancestor_inverse, rows_float), 'row', scatter_d...  99.9 us
    dot_general x14, matrix products, matmul(): return jnp.dot(left, right, precision=highest)  96.3 us
    psum x1, waiting for transfers between devices, broadcast(): return lax.psum(kept, axis)  92.8 us
    dot_general x9, matrix products, left_dot(): lax.dot_general(left, right, (((0,), (0,)), ((), ())), precision=highest)  80.7 us
  transfers between devices with their start and end apart: 11, of which 11 were waited for; matrix products, arithmetic and copies ran while one was open for 15% of the time, Pallas kernels for 0%

commit v1 on v0

--- a/solution.py
+++ b/solution.py
@@ -53,7 +53,7 @@
             )
         column = -product_sum
         stacked = jnp.concatenate(row_layout + [column], axis=1)
-        summed = lax.psum(left_dot(lower_here, stacked), ("row", "col"))
+        summed = lax.psum(lax.psum(left_dot(lower_here, stacked), "row"), "col")
         crosses = [
             summed[:, earlier * sn_width : (earlier + 1) * sn_width] for earlier in range(current)
         ]

time: 1020 us -> 1200 us (1.18)
  waiting for transfers between devices: 754 us -> 937 us
    psum x1 -> x2, waiting for transfers between devices: 147 us -> 254 us  [local(): summed = lax.psum(lax.psum(left_dot(lower_here, stacked), 'row'), 'col')]
    reduce_scatter x3, waiting for transfers between devices: 236 us -> 299 us  [local(): lax.psum_scatter(matmul(ancestor_inverse, lower_cols), 'col', scatter_dim...]
    reduce_scatter x3, waiting for transfers between devices: 99.9 us -> 113 us  [local(): lax.psum_scatter(left_dot(ancestor_inverse, rows_float), 'row', scatter_d...]
  transfers between devices with their start and end apart: 11 -> 12, of which waited for: 11 -> 12; matrix products, arithmetic and copies ran while one was open for 15% -> 12% of each run, Pallas kernels for 0% -> 0%
where the time goes in v1:
time: 1200 us
  waiting for transfers between devices  937 us (78%)
  matrix products  180 us (15%)
  other arithmetic  31.1 us (3%)
  local copies, waits for them, and re-layouts  19.7 us (2%)
  between operations  15 us (1%)
  starting transfers between devices  12.7 us (1%)
    reduce_scatter x3, waiting for transfers between devices, local(): lax.psum_scatter(matmul(ancestor_inverse, lower_cols), 'col', scatter_dim...  299 us
    psum x2, waiting for transfers between devices, local(): summed = lax.psum(lax.psum(left_dot(lower_here, stacked), 'row'), 'col')  254 us
    all_gather x3, waiting for transfers between devices, local(): lower_rows = lax.all_gather(lower_part, 'col', axis=0, tiled=True)  177 us
    reduce_scatter x3, waiting for transfers between devices, local(): lax.psum_scatter(left_dot(ancestor_inverse, rows_float), 'row', scatter_d...  113 us
    dot_general x14, matrix products, matmul(): return jnp.dot(left, right, precision=highest)  97.1 us
    psum x1, waiting for transfers between devices, broadcast(): return lax.psum(kept, axis)  92.8 us
    dot_general x9, matrix products, left_dot(): lax.dot_general(left, right, (((0,), (0,)), ((), ())), precision=highest)  82.4 us
  transfers between devices with their start and end apart: 12, of which 12 were waited for; matrix products, arithmetic and copies ran while one was open for 12% of the time, Pallas kernels for 0%

profile of v1, /device:TPU:0, one launch (start us, length us, event | category | flops | bytes accessed | tf_op | source)
XLA Modules:
  0.0 1195.5 jit_solution(811163514902072832)
XLA Ops:
  8.1 2.5 bitcast_select_fusion.1
  12.2 61.3 %all-gather.8.cloned.1.call-done = bf16[3072,512]{1,0:T(8,128)(2,1)} async-done(((bf16[384,512]{1,0:T(8,128)(2,1)}), bf16[3072,512]{1,0:T(8,128)(2,1)}) %all-gather.8.cloned.1.call-update) | async-done | bytes 3145744 | tf_op jit(solution)/shard_map/all_gather | solution.py:43
  73.5 2.8 dynamic-slice_select_fusion
  76.3 58.1 %all-gather.4.cloned.1.call-done = bf16[3072,512]{1,0:T(8,128)(2,1)} async-done(((bf16[384,512]{1,0:T(8,128)(2,1)}), bf16[3072,512]{1,0:T(8,128)(2,1)}) %all-gather.4.cloned.1.call-update) | async-done | bytes 3145744 | tf_op jit(solution)/shard_map/all_gather | solution.py:43
  134.4 2.8 dynamic-slice_select_fusion.2
  137.2 58.1 %all-gather.6.cloned.1.call-done = bf16[3072,512]{1,0:T(8,128)(2,1)} async-done(((bf16[384,512]{1,0:T(8,128)(2,1)}), bf16[3072,512]{1,0:T(8,128)(2,1)}) %all-gather.6.cloned.1.call-update) | async-done | bytes 3145744 | tf_op jit(solution)/shard_map/all_gather | solution.py:43
  195.3 2.8 dynamic-slice_select_fusion.1
  198.2 92.8 %all-reduce.11.cloned.1.call-done = (bf16[1536,512]{1,0:T(8,128)(2,1)}, bf16[1536,512]{1,0:T(8,128)(2,1)}, bf16[1536,512]{1,0:T(8,128)(2,1)}) async-done(((bf16[1536,512]{1,0:T(8,128)(2,1)}, bf16[1536,512]{1,0:T(8,128)(2,1)}, bf16[1536,512]{1,0:T(8,128)(2,1)}), (bf16[1536,512]{1,0:T(8,128)(2,1)}, bf16[1536,512]{1,0:T(8,128)(2,1)}, bf16[1536,512]{1,0:T(8,128)(2,1)})) %all-reduce.11.cloned.1.call-update) | async-done | bytes 4718608 | tf_op jit(solution)/shard_map/psum | solution.py:11
  291.0 22.2 %convolution_bitcast_fusion = f32[3072,512]{0,1:T(8,128)} fusion(bf16[1536,512]{1,0:T(8,128)(2,1)} %get-tuple-element.18, f32[3072,1536]{1,0:T(8,128)} %param.5), kind=kOutput, calls=%fused_computation.1 | convolution fusion | flops 28991029248 | bytes 26738688 | tf_op jit(solution)/shard_map/dot_general | solution.py:15
  314.7 21.8 %convolution_bitcast_fusion.2 = f32[3072,512]{0,1:T(8,128)} fusion(bf16[1536,512]{1,0:T(8,128)(2,1)S(1)} %copy-done.26, f32[3072,1536]{1,0:T(8,128)} %param.5), kind=kOutput, calls=%fused_computation.3 | convolution fusion | flops 28991029248 | bytes 26738688 | tf_op jit(solution)/shard_map/dot_general | solution.py:15
  336.5 11.7 reduce-scatter.9.cloned.1.call-start
  348.3 21.9 %convolution_bitcast_fusion.1 = f32[3072,512]{0,1:T(8,128)} fusion(bf16[1536,512]{1,0:T(8,128)(2,1)S(1)} %copy-done.25, f32[3072,1536]{1,0:T(8,128)} %param.5), kind=kOutput, calls=%fused_computation.2 | convolution fusion | flops 28991029248 | bytes 26738688 | tf_op jit(solution)/shard_map/dot_general | solution.py:15
  370.2 61.4 %reduce-scatter.11.cloned.1.call-done = f32[384,512]{0,1:T(8,128)} async-done(((f32[3072,512]{0,1:T(8,128)}), f32[384,512]{0,1:T(8,128)}) %reduce-scatter.11.cloned.1.call-update) | async-done | bytes 786448 | tf_op jit(solution)/shard_map/reduce_scatter | solution.py:47
  431.6 120.7 %reduce-scatter.7.cloned.1.call-done = f32[384,512]{0,1:T(8,128)} async-done(((f32[3072,512]{0,1:T(8,128)}), f32[384,512]{0,1:T(8,128)}) %reduce-scatter.7.cloned.1.call-update) | async-done | bytes 786448 | tf_op jit(solution)/shard_map/reduce_scatter | solution.py:47
  552.4 4.1 convolution_add_fusion.4
  556.5 116.8 %reduce-scatter.9.cloned.1.call-done = f32[384,512]{0,1:T(8,128)} async-done(((f32[3072,512]{0,1:T(8,128)}), f32[384,512]{0,1:T(8,128)}) %reduce-scatter.9.cloned.1.call-update) | async-done | bytes 786448 | tf_op jit(solution)/shard_map/reduce_scatter | solution.py:47
  673.3 3.3 fusion.14
  679.5 3.1 fusion.6
  682.7 4.5 fusion
  687.1 2.1 fusion.64
  689.7 20.7 %convolution_bitcast_fusion.3 = f32[1536,512]{0,1:T(8,128)} fusion(bf16[3072,512]{1,0:T(8,128)(2,1)} %all-gather.8.cloned.1.call-done, f32[3072,1536]{1,0:T(8,128)} %param.5), kind=kOutput, calls=%fused_computation.4 | convolution fusion | flops 28991029248 | bytes 25165824 | tf_op jit(solution)/shard_map/dot_general | solution.py:19
  710.5 20.8 %convolution_bitcast_fusion.5 = f32[1536,512]{0,1:T(8,128)} fusion(bf16[3072,512]{1,0:T(8,128)(2,1)} %all-gather.4.cloned.1.call-done, f32[3072,1536]{1,0:T(8,128)} %param.5), kind=kOutput, calls=%fused_computation.6 | convolution fusion | flops 28991029248 | bytes 25165824 | tf_op jit(solution)/shard_map/dot_general | solution.py:19
  731.5 20.7 %convolution_bitcast_fusion.4 = f32[1536,512]{0,1:T(8,128)} fusion(bf16[3072,512]{1,0:T(8,128)(2,1)} %all-gather.6.cloned.1.call-done, f32[3072,1536]{1,0:T(8,128)} %param.5), kind=kOutput, calls=%fused_computation.5 | convolution fusion | flops 28991029248 | bytes 25165824 | tf_op jit(solution)/shard_map/dot_general | solution.py:19
  752.3 56.0 %all-reduce.9.cloned.1.call-done = (f32[512,1536]{1,0:T(8,128)}, f32[512,512]{1,0:T(8,128)}, f32[512,1024]{0,1:T(8,128)}) async-done(((f32[512,1536]{1,0:T(8,128)}, f32[512,512]{1,0:T(8,128)}, f32[512,1024]{0,1:T(8,128)}), (f32[512,1536]{1,0:T(8,128)}, f32[512,512]{1,0:T(8,128)}, f32[512,1024]{0,1:T(8,128)})) %all-reduce.9.cloned.1.call-update) | async-done | bytes 6291472 | tf_op jit(solution)/shard_map/psum | solution.py:56
  808.3 2.3 slice.74
  810.6 2.5 copy.65
  813.1 36.2 %reduce-scatter.17.cloned.1.call-done = f32[384,512]{0,1:T(8,128)} async-done(((f32[1536,512]{0,1:T(8,128)}), f32[384,512]{0,1:T(8,128)}) %reduce-scatter.17.cloned.1.call-update) | async-done | bytes 786448 | tf_op jit(solution)/shard_map/reduce_scatter | solution.py:76
  849.4 40.1 %reduce-scatter.13.cloned.1.call-done = f32[384,512]{0,1:T(8,128)} async-done(((f32[1536,512]{0,1:T(8,128)}), f32[384,512]{0,1:T(8,128)}) %reduce-scatter.13.cloned.1.call-update) | async-done | bytes 786448 | tf_op jit(solution)/shard_map/reduce_scatter | solution.py:76
  889.5 4.1 convolution_add_fusion.1
  893.6 36.2 %reduce-scatter.15.cloned.1.call-done = f32[384,512]{0,1:T(8,128)} async-done(((f32[1536,512]{0,1:T(8,128)}), f32[384,512]{0,1:T(8,128)}) %reduce-scatter.15.cloned.1.call-update) | async-done | bytes 786448 | tf_op jit(solution)/shard_map/reduce_scatter | solution.py:76
  929.8 3.4 fusion.16
  936.7 3.1 copy.51
  939.8 3.2 pad_maximum_fusion.1
  943.0 3.2 copy.50
  946.3 198.1 %all-reduce.7.cloned.1.call-done = (f32[512,1536]{1,0:T(8,128)}, f32[512,512]{1,0:T(8,128)}, f32[512,1024]{0,1:T(8,128)}) async-done(((f32[512,1536]{1,0:T(8,128)}, f32[512,512]{1,0:T(8,128)}, f32[512,1024]{0,1:T(8,128)}), (f32[512,1536]{1,0:T(8,128)}, f32[512,512]{1,0:T(8,128)}, f32[512,1024]{0,1:T(8,128)})) %all-reduce.7.cloned.1.call-update) | async-done | bytes 6291472 | tf_op jit(solution)/shard_map/psum | solution.py:56
  1144.3 3.6 fusion.34
  1148.0 3.2 bitcast_subtract_fusion.7
  1151.2 1.9 fusion.32
  1155.0 2.0 fusion.13
  1159.9 3.3 fusion.12
  1163.2 2.3 fusion.20
  1165.5 2.3 fusion.70
  1167.8 2.6 copy.39
  1170.4 5.3 fusion.11
  1175.7 2.0 maximum_bitcast_fusion.1
  1177.7 2.4 copy.49
  1180.1 2.3 maximum_bitcast_fusion.2
  1183.2 5.1 pad_maximum_fusion
  (88 shorter events, 16.7 us)
Async XLA Ops:
  7.2 66.3 %all-gather.8.cloned.1.call-start = ((), (), s32[]{:S(2)}) async-start(), calls=%async_computation.10 | async-start | bytes 3538944 | tf_op jit(solution)/shard_map/all_gather | solution.py:43
  10.6 123.8 %all-gather.4.cloned.1.call-start = ((), (), s32[]{:S(2)}) async-start(), calls=%async_computation.6 | async-start | bytes 3538944 | tf_op jit(solution)/shard_map/all_gather | solution.py:43
  11.4 183.9 %all-gather.6.cloned.1.call-start = ((), (), s32[]{:S(2)}) async-start(), calls=%async_computation.8 | async-start | bytes 3538944 | tf_op jit(solution)/shard_map/all_gather | solution.py:43
  12.1 278.9 %all-reduce.11.cloned.1.call-start = ((), (), s32[]{:S(2)}) async-start(), calls=%async_computation.17 | async-start | bytes 9437184 | tf_op jit(solution)/shard_map/psum | solution.py:11
  198.2 233.5 %reduce-scatter.11.cloned.1.call-start = ((), (), s32[]{:S(2)}) async-start(), calls=%async_computation.11 | async-start | bytes 7077888 | tf_op jit(solution)/shard_map/reduce_scatter | solution.py:47
  313.3 1.4 copy-start.26
  313.3 239.1 %reduce-scatter.7.cloned.1.call-start = ((), (), s32[]{:S(2)}) async-start(), calls=%async_computation.7 | async-start | bytes 7077888 | tf_op jit(solution)/shard_map/reduce_scatter | solution.py:47
  336.5 11.7 copy-start.25
  336.5 336.7 %reduce-scatter.9.cloned.1.call-start = ((), (), s32[]{:S(2)}) async-start(), calls=%async_computation.9 | async-start | bytes 7077888 | tf_op jit(solution)/shard_map/reduce_scatter | solution.py:47
  370.2 182.2 %copy-start = (f32[3,512,512]{2,1,0:T(8,128)S(1)}, f32[3,512,512]{2,1,0:T(8,128)}, u32[]{:S(2)}) copy-start(f32[3,512,512]{2,1,0:T(8,128)} %param.7) | copy-start | bytes 9437188
  370.2 438.1 %all-reduce.9.cloned.1.call-start = ((), (), s32[]{:S(2)}) async-start(), calls=%async_computation.16 | async-start | bytes 12582912 | tf_op jit(solution)/shard_map/psum | solution.py:56
  673.3 3.4 copy-start.23
  673.3 5.3 copy-start.7
  676.6 6.0 copy-start.3
  676.6 2.9 copy-start.22
  678.5 4.1 copy-start.12
  678.5 4.1 copy-start.14
  682.7 4.5 copy-start.21
  689.3 160.1 %reduce-scatter.17.cloned.1.call-start = ((), (), s32[]{:S(2)}) async-start(), calls=%async_computation.14 | async-start | bytes 3932160 | tf_op jit(solution)/shard_map/reduce_scatter | solution.py:76
  710.4 179.1 %reduce-scatter.13.cloned.1.call-start = ((), (), s32[]{:S(2)}) async-start(), calls=%async_computation.12 | async-start | bytes 3932160 | tf_op jit(solution)/shard_map/reduce_scatter | solution.py:76
  731.3 198.5 %reduce-scatter.15.cloned.1.call-start = ((), (), s32[]{:S(2)}) async-start(), calls=%async_computation.13 | async-start | bytes 3932160 | tf_op jit(solution)/shard_map/reduce_scatter | solution.py:76
  752.2 392.1 %all-reduce.7.cloned.1.call-start = ((), (), s32[]{:S(2)}) async-start(), calls=%async_computation.15 | async-start | bytes 12582912 | tf_op jit(solution)/shard_map/psum | solution.py:56
  929.8 3.4 copy-start.24
  929.8 5.3 copy-start.13
  1144.3 3.6 copy-start.10
  1144.3 3.6 copy-start.11
  1151.1 3.8 copy-start.1
  1151.1 3.8 copy-start.15
  1151.1 3.8 copy-start.16
  1153.1 12.4 %copy-start.4 = (f32[512,512]{0,1:T(8,128)}, f32[512,512]{0,1:T(8,128)S(1)}, u32[]{:S(2)}) copy-start(f32[512,512]{0,1:T(8,128)S(1)} %fusion.32) | copy-start | bytes 3145732
  1155.0 4.9 copy-start.6
  1157.0 1.0 copy-start.8
  1159.9 5.6 copy-start.5
  1170.4 5.3 copy-start.9
  1170.4 5.3 copy-start.19
  1170.4 5.3 copy-start.20
  1180.0 2.4 copy-start.2
  1180.1 2.5 copy-start.17
  1180.1 2.8 copy-start.18
Sparse Core Ops, SparseCore 0:
  10.7 62.7 all-gather.7
  75.7 58.6 all-gather.3
  136.6 58.6 all-gather.5
  198.3 92.7 all-reduce.10
  313.4 118.1 reduce-scatter.10
  435.1 117.2 reduce-scatter.6
  556.0 117.2 reduce-scatter.8
  689.4 118.8 all-reduce.8
  811.4 37.9 reduce-scatter.16
  851.7 37.7 reduce-scatter.12
  892.0 37.7 reduce-scatter.14
  933.9 210.3 all-reduce.6
